TPU v7x, 32 devices: a whole 2x2x4 slice. The times are simulated.
32 devices in a mesh: row: 4 (over y, x), col: 8 (over z, core).
Axes of the slice: x: 2, y: 2, z: 4, core: 2. Of those that a mesh axis runs over, the one named last changes fastest.
Arguments:
- vectors: bfloat16 [64, 131072], P(None, ('col', 'row')), may hold values from -6 to 6
- blocks: bfloat16 [4, 4096, 128, 128], P('row', 'col'), may hold values from -0.1875 to 0.1875
- block_rows: int32 [4, 4096], P('row', 'col'), may hold values from 0 to 255, as said below
- block_cols: int32 [4, 4096], P('row', 'col'), may hold values from 0 to 127, as said below
- counts: int32 [4, 8], P('row', 'col'), may hold values from 1 to 512, as said below
Outputs:
- result: float32 [64, 131072], P(None, ('row', 'col'))
Inputs may be any that keep to these rules, and one draw needn't show every extreme that they name: Within one owner pair the slots below its count name distinct positions (block_rows, block_cols) of its 256 x 256/2 grid of blocks; later slots hold 0. `block_cols`: see block_rows. `counts`: some owner pair holds exactly 512 blocks, and some other exactly one.
All inputs are finite; a program needn't handle non-finite values.
Results may differ from a plain program's by a relative error of at most 0.0029.
Values may be sent and summed in bfloat16 or wider, within the bound.
No kernel may reach another device: no remote copies, remote signals or barrier semaphores. Data moves between devices by JAX's collectives and lax.ppermute only.
A program may use at most 128 MiB of HBM per device.

v0:
```python
import jax
import jax.numpy as jnp
from jax import lax
from jax.sharding import PartitionSpec as P


def from_root(block, axis, owner):
    block = jnp.where(lax.axis_index(axis) == owner, block, jnp.zeros_like(block))
    return lax.psum(block, axis)


def block_product(vec_panel, blocks, block_rows, block_cols, counts):
    slot_total = blocks.shape[1]
    tile_size = blocks.shape[2]
    vec_width = vec_panel.shape[0]
    row_blocks = 2 * vec_panel.shape[1] // tile_size
    vec_tiles = vec_panel.reshape(vec_width, -1, tile_size)
    picked = jnp.take(vec_tiles, block_cols.reshape(-1), axis=1)
    product = jnp.einsum("ksc,src->ksr", picked, blocks[0], preferred_element_type=jnp.float32)
    live_slots = jnp.arange(slot_total, dtype=jnp.int32) < counts.reshape(())
    owner_map = (block_rows == jnp.arange(row_blocks, dtype=jnp.int32)[:, None]) & live_slots[
        None, :
    ]
    summed = jnp.einsum(
        "is,ksr->kir", owner_map.astype(jnp.float32), product, precision=lax.Precision.HIGHEST
    )
    return summed.reshape(vec_width, row_blocks * tile_size)


def relay_group(group_rows):
    half_width = group_rows.shape[1] // 2
    col_owner = lax.axis_index("col")
    own_half = lax.dynamic_slice_in_dim(group_rows, col_owner % 2 * half_width, half_width, 1)
    return from_root(own_half, "row", col_owner // 2)


def shards(vectors, blocks, block_rows, block_cols, counts):
    vec_panel = lax.all_gather(vectors, "row", axis=1, tiled=True)
    first_part = block_product(vec_panel, blocks, block_rows, block_cols, counts)
    group_rows = lax.psum(first_part, "col").astype(jnp.bfloat16)
    second_panel = relay_group(group_rows)
    second_part = block_product(second_panel, blocks, block_rows, block_cols, counts)
    return lax.psum_scatter(second_part, "col", scatter_dimension=1, tiled=True)


def solution(mesh):
    in_specs = (
        P(None, ("col", "row")),
        P("row", "col", None, None),
        P("row", "col"),
        P("row", "col"),
        P("row", "col"),
    )
    out_specs = P(None, ("row", "col"))
    return jax.shard_map(shards, mesh=mesh, in_specs=in_specs, out_specs=out_specs, check_vma=False)
```

profile of v0, /device:TPU:0, one launch (start us, length us, event | category | flops | bytes accessed | tf_op | source)
XLA Modules:
  0.0 559.0 jit_solution(10236251056222093758)
XLA Ops:
  6.5 0.7 all-gather.2.cloned.1.call-update
  7.3 0.0 all-reduce.3.cloned.1.call-start
  8.0 0.7 compare_select_fusion
  8.7 0.7 compare_and_fusion
  9.4 37.7 %all-gather.2.cloned.1.call-done = bf16[64,16384]{1,0:T(8,128)(2,1)} async-done(((bf16[64,4096]{1,0:T(8,128)(2,1)}), bf16[64,16384]{1,0:T(8,128)(2,1)}) %all-gather.2.cloned.1.call-update) | async-done | bytes 2097168 | tf_op jit(solution)/shard_map/all_gather | solution.py:38
  47.1 2.2 copy_bitcast_fusion.3
  49.3 13.5 %gather_fusion = bf16[512,64,128]{2,1,0:T(8,128)(2,1)} fusion(bf16[64,128,128]{2,0,1:T(8,128)(2,1)S(1)} %copy_bitcast_fusion.3, s32[1024]{0:T(1024)S(1)} %pad_clamp_fusion), kind=kCustom, calls=%fused_computation.clone | custom fusion | bytes 16779264 | tf_op jit(solution)/shard_map/jit(_take)/gather | solution.py:18
  62.8 20.4 %fusion.8 = f32[64,512,128]{2,0,1:T(8,128)} fusion(bf16[1,512,128,128]{3,2,1,0:T(8,128)(2,1)} %param.8, bf16[512,64,128]{2,1,0:T(8,128)(2,1)} %gather_fusion, pred[512]{0:T(512)(128)(4,1)S(1)} %compare_and_fusion), kind=kOutput, calls=%fused_computation.10 | convolution fusion | flops 1077936128 | bytes 41943552 | tf_op jit(solution)/shard_map/ksc,src->ksr/dot_general | solution.py:19
  83.2 0.0 copy-done
  83.2 27.8 %fusion.22 = f32[64,256,128]{1,2,0:T(8,128)} fusion(f32[64,512,128]{2,0,1:T(8,128)} %fusion.8, s32[512]{0:T(512)S(1)} %bitcast.53, pred[512]{0:T(512)(128)(4,1)S(1)} %iota_compare_fusion.1), kind=kOutput, calls=%fused_computation.23 | convolution fusion | flops 12885164032 | bytes 25168384 | tf_op jit(solution)/shard_map/is,ksr->kir/dot_general | solution.py:24
  111.0 9.2 %copy.10 = f32[64,256,128]{2,1,0:T(8,128)} copy(f32[64,256,128]{1,2,0:T(8,128)} %fusion.22) | data formatting | bytes 16777216 | tf_op jit(solution)/shard_map/is,ksr->kir/transpose | solution.py:24
  120.2 11.3 %copy.31 = f32[8,8,256,128]{3,1,2,0:T(8,128)} copy(f32[8,8,256,128]{3,2,1,0:T(8,128)} %bitcast.50) | data formatting | bytes 16777216
  131.5 170.1 %all-reduce.4 = bf16[64,32768]{1,0:T(8,128)(2,1)} all-reduce(f32[64,32768]{1,0:T(8,128)} %bitcast.51), channel_id=1, replica_groups=mesh['row'=4,'col'=8] {'col'}, use_global_device_ids=true, to_apply=%region_0.0 | all-reduce | flops 2097152 | bytes 12582912 | tf_op jit(solution)/shard_map/psum | solution.py:40
  301.6 3.5 copy_bitcast_fusion.2
  305.1 0.0 all-reduce.3.cloned.1.call-update
  305.1 0.0 reduce-scatter.2.cloned.1.call-start
  305.2 67.0 %all-reduce.3.cloned.1.call-done = bf16[64,128,128]{2,0,1:T(8,128)(2,1)} async-done(((bf16[64,128,128]{2,0,1:T(8,128)(2,1)}), bf16[64,128,128]{2,0,1:T(8,128)(2,1)}) %all-reduce.3.cloned.1.call-update) | async-done | bytes 2097168 | tf_op jit(solution)/shard_map/psum | solution.py:9
  372.2 21.6 %gather_fusion.1 = bf16[512,64,128]{2,1,0:T(8,128)(2,1)} fusion(bf16[64,128,128]{2,0,1:T(8,128)(2,1)} %all-reduce.3.cloned.1.call-done, s32[1024]{0:T(1024)S(1)} %pad_clamp_fusion), kind=kCustom, calls=%fused_computation.1.clone | custom fusion | bytes 16779264 | tf_op jit(solution)/shard_map/jit(_take)/gather | solution.py:18
  393.8 20.5 %fusion.11 = f32[64,512,128]{2,0,1:T(8,128)} fusion(bf16[1,512,128,128]{3,2,1,0:T(8,128)(2,1)} %param.8, bf16[512,64,128]{2,1,0:T(8,128)(2,1)} %gather_fusion.1, pred[512]{0:T(512)(128)(4,1)S(1)} %compare_and_fusion), kind=kOutput, calls=%fused_computation.11 | convolution fusion | flops 1077936128 | bytes 41943552 | tf_op jit(solution)/shard_map/ksc,src->ksr/dot_general | solution.py:19
  414.3 27.8 %fusion.25 = f32[64,256,128]{1,2,0:T(8,128)} fusion(f32[64,512,128]{2,0,1:T(8,128)} %fusion.11, s32[512]{0:T(512)S(1)} %bitcast.54, pred[512]{0:T(512)(128)(4,1)S(1)} %iota_compare_fusion.1), kind=kOutput, calls=%fused_computation.24 | convolution fusion | flops 12885164032 | bytes 25168384 | tf_op jit(solution)/shard_map/is,ksr->kir/dot_general | solution.py:24
  442.0 9.2 %copy.13 = f32[64,256,128]{2,1,0:T(8,128)} copy(f32[64,256,128]{1,2,0:T(8,128)} %fusion.25) | data formatting | bytes 16777216 | tf_op jit(solution)/shard_map/is,ksr->kir/transpose | solution.py:24
  451.2 11.3 %copy.30 = f32[8,8,256,128]{3,1,2,0:T(8,128)} copy(f32[8,8,256,128]{3,2,1,0:T(8,128)} %bitcast.52) | data formatting | bytes 16777216
  462.5 0.0 reduce-scatter.2.cloned.1.call-update
  462.6 89.7 %reduce-scatter.2.cloned.1.call-done = f32[64,4096]{1,0:T(8,128)} async-done(((f32[64,32768]{1,0:T(8,128)}), f32[64,4096]{1,0:T(8,128)}) %reduce-scatter.2.cloned.1.call-update) | async-done | bytes 1048592 | tf_op jit(solution)/shard_map/reduce_scatter | solution.py:43
  (4 shorter events, 0.0 us)
Async XLA Ops:
  6.5 40.6 %all-gather.2.cloned.1.call-start = ((), (), s32[]{:S(2)}) async-start(), calls=%async_computation.1 | async-start | bytes 2621440 | tf_op jit(solution)/shard_map/all_gather | solution.py:38
  7.3 364.9 %all-reduce.3.cloned.1.call-start = ((), (), s32[]{:S(2)}) async-start(), calls=%async_computation.2 | async-start | bytes 4194304 | tf_op jit(solution)/shard_map/psum | solution.py:9
  62.8 20.5 %copy-start = (s32[1,512]{1,0:T(1,128)S(1)}, s32[1,512]{1,0:T(1,128)}, u32[]{:S(2)}) copy-start(s32[1,512]{1,0:T(1,128)} %param.9) | copy-start | bytes 6148
  305.1 247.1 %reduce-scatter.2.cloned.1.call-start = ((), (), s32[]{:S(2)}) async-start(), calls=%async_computation.3 | async-start | bytes 9437184 | tf_op jit(solution)/shard_map/reduce_scatter | solution.py:43
Sparse Core Ops, SparseCore 0:
  9.2 37.8 all-gather.1
  305.3 66.8 all-reduce.2
  462.7 89.5 reduce-scatter.1
where the time goes:
time: 565 us; the launch traced here: 559 us
  waiting for transfers between devices  195 us (35%)
  blocking collectives  170 us (30%)
  matrix products  96.5 us (17%)
  local copies, waits for them, and re-layouts  78.3 us (14%)
  between operations  14 us (2%)
    psum x1, blocking collectives, shards(): group_rows = lax.psum(first_part, 'col').astype(jnp.bfloat16)  170 us
    reduce_scatter x1, waiting for transfers between devices, shards(): return lax.psum_scatter(second_part, 'col', scatter_dimension=1, tiled=True)  89.7 us
    psum x1, waiting for transfers between devices, from_root(): return lax.psum(block, axis)  67 us
    dot_general x2, matrix products, block_product(): jnp.einsum('is,ksr->kir', owner_map.astype(jnp.float32), product, precisi...  55.6 us
    dot_general x2, matrix products, block_product(): jnp.einsum('ksc,src->ksr', picked, blocks[0], preferred_element_type=jnp....  40.9 us
    all_gather x1, waiting for transfers between devices, shards(): vec_panel = lax.all_gather(vectors, 'row', axis=1, tiled=True)  37.7 us
    gather x2, local copies, waits for them, and re-layouts, block_product(): picked = jnp.take(vec_tiles, block_cols.reshape(-1), axis=1)  35.1 us
    unnamed x4, local copies, waits for them, and re-layouts  22.7 us
  transfers between devices with their start and end apart: 3, of which 3 were waited for; matrix products, arithmetic and copies ran while one was open for 0% of the time, Pallas kernels for 0%

commit v1 on v0

--- a/solution.py
+++ b/solution.py
@@ -35,7 +35,14 @@
 
 
 def shards(vectors, blocks, block_rows, block_cols, counts):
-    vec_panel = lax.all_gather(vectors, "row", axis=1, tiled=True)
+    ways, here, step = (lax.axis_size("row"), lax.axis_index("row"), vectors.shape[1])
+    line, have = (vectors, 1)
+    while have < ways:
+        line = jnp.concatenate(
+            [line, lax.ppermute(line, "row", [(d, (d - have) % ways) for d in range(ways)])], axis=1
+        )
+        have = 2 * have
+    vec_panel = jnp.roll(line, here * step, axis=1)
     first_part = block_product(vec_panel, blocks, block_rows, block_cols, counts)
     group_rows = lax.psum(first_part, "col").astype(jnp.bfloat16)
     second_panel = relay_group(group_rows)

time: 565 us -> 568 us (level)
    all_gather x1 -> x0, waiting for transfers between devices: 37.7 us -> none  [shards(): vec_panel = lax.all_gather(vectors, 'row', axis=1, tiled=True)]
    ppermute x0 -> x2, waiting for transfers between devices: none -> 30.9 us  [shards(): lax.ppermute(line, 'row', [(d, (d - have) % ways) for d in range(ways)])]
    unnamed x4 -> x9, local copies, waits for them, and re-layouts: 22.7 us -> 24.9 us
  transfers between devices with their start and end apart: 3 -> 4, of which waited for: 3 -> 4; matrix products, arithmetic and copies ran while one was open for 0% -> 0% of each run, Pallas kernels for 0% -> 0%
where the time goes in v1:
time: 568 us; the launch traced here: 561 us
  waiting for transfers between devices  191 us (34%)
  blocking collectives  169 us (30%)
  matrix products  96.5 us (17%)
  local copies, waits for them, and re-layouts  79.1 us (14%)
  between operations  14.4 us (3%)
  other arithmetic  6.01 us (1%)
    psum x1, blocking collectives, shards(): group_rows = lax.psum(first_part, 'col').astype(jnp.bfloat16)  169 us
    reduce_scatter x1, waiting for transfers between devices, shards(): return lax.psum_scatter(second_part, 'col', scatter_dimension=1, tiled=True)  89.7 us
    psum x1, waiting for transfers between devices, from_root(): return lax.psum(block, axis)  70 us
    dot_general x2, matrix products, block_product(): jnp.einsum('is,ksr->kir', owner_map.astype(jnp.float32), product, precisi...  55.6 us
    dot_general x2, matrix products, block_product(): jnp.einsum('ksc,src->ksr', picked, blocks[0], preferred_element_type=jnp....  40.9 us
    gather x2, local copies, waits for them, and re-layouts, block_product(): picked = jnp.take(vec_tiles, block_cols.reshape(-1), axis=1)  35.1 us
    ppermute x2, waiting for transfers between devices, shards(): lax.ppermute(line, 'row', [(d, (d - have) % ways) for d in range(ways)])  30.9 us
    unnamed x9, local copies, waits for them, and re-layouts  24.9 us
  transfers between devices with their start and end apart: 4, of which 4 were waited for; matrix products, arithmetic and copies ran while one was open for 0% of the time, Pallas kernels for 0%

profile of v1, /device:TPU:0, one launch (start us, length us, event | category | flops | bytes accessed | tf_op | source)
XLA Modules:
  0.0 560.8 jit_solution(15833295295872210940)
XLA Ops:
  6.5 3.9 collective-permute-start
  11.1 0.7 compare_and_fusion
  11.8 0.7 compare_select_fusion
  12.5 9.5 %collective-permute-done = bf16[64,4096]{1,0:T(8,128)(2,1)S(1)} collective-permute-done((bf16[64,4096]{1,0:T(8,128)(2,1)}, bf16[64,4096]{1,0:T(8,128)(2,1)S(1)}, u32[]{:S(2)}, u32[]{:S(2)}) %collective-permute-start) | collective-permute-done | bytes 524320 | tf_op jit(solution)/shard_map/ppermute | solution.py:42
  22.0 1.1 pad_maximum_fusion
  23.1 1.5 collective-permute-start.1
  24.6 1.1 constant_dynamic-update-slice_fusion.5
  25.7 21.5 %collective-permute-done.1 = bf16[64,8192]{1,0:T(8,128)(2,1)S(1)} collective-permute-done((bf16[64,8192]{1,0:T(8,128)(2,1)S(1)}, bf16[64,8192]{1,0:T(8,128)(2,1)S(1)}, u32[]{:S(2)}, u32[]{:S(2)}) %collective-permute-start.1) | collective-permute-done | bytes 1048608 | tf_op jit(solution)/shard_map/ppermute | solution.py:42
  47.3 1.1 constant_dynamic-update-slice_fusion.2
  48.5 0.6 copy_bitcast_fusion.3
  49.1 13.5 %gather_fusion = bf16[512,64,128]{2,1,0:T(8,128)(2,1)} fusion(bf16[64,128,128]{2,0,1:T(8,128)(2,1)S(1)} %copy_bitcast_fusion.3, s32[1024]{0:T(1024)S(1)} %pad_clamp_fusion), kind=kCustom, calls=%fused_computation.clone | custom fusion | bytes 16779264 | tf_op jit(solution)/shard_map/jit(_take)/gather | solution.py:18
  62.5 20.4 %fusion.8 = f32[64,512,128]{2,0,1:T(8,128)} fusion(bf16[1,512,128,128]{3,2,1,0:T(8,128)(2,1)} %param.8, bf16[512,64,128]{2,1,0:T(8,128)(2,1)} %gather_fusion, pred[512]{0:T(512)(128)(4,1)S(1)} %compare_and_fusion), kind=kOutput, calls=%fused_computation.10 | convolution fusion | flops 1077936128 | bytes 41943552 | tf_op jit(solution)/shard_map/ksc,src->ksr/dot_general | solution.py:19
  83.0 27.8 %fusion.22 = f32[64,256,128]{1,2,0:T(8,128)} fusion(f32[64,512,128]{2,0,1:T(8,128)} %fusion.8, s32[512]{0:T(512)S(1)} %bitcast.53, pred[512]{0:T(512)(128)(4,1)S(1)} %iota_compare_fusion.1), kind=kOutput, calls=%fused_computation.23 | convolution fusion | flops 12885164032 | bytes 25168384 | tf_op jit(solution)/shard_map/is,ksr->kir/dot_general | solution.py:24
  110.8 9.2 %copy.10 = f32[64,256,128]{2,1,0:T(8,128)} copy(f32[64,256,128]{1,2,0:T(8,128)} %fusion.22) | data formatting | bytes 16777216 | tf_op jit(solution)/shard_map/is,ksr->kir/transpose | solution.py:24
  120.0 11.3 %copy.31 = f32[8,8,256,128]{3,1,2,0:T(8,128)} copy(f32[8,8,256,128]{3,2,1,0:T(8,128)} %bitcast.50) | data formatting | bytes 16777216
  131.3 168.8 %all-reduce.4 = bf16[64,32768]{1,0:T(8,128)(2,1)} all-reduce(f32[64,32768]{1,0:T(8,128)} %bitcast.51), channel_id=1, replica_groups=mesh['row'=4,'col'=8] {'col'}, use_global_device_ids=true, to_apply=%region_0.2 | all-reduce | flops 2097152 | bytes 12582912 | tf_op jit(solution)/shard_map/psum | solution.py:47
  300.1 3.5 copy_bitcast_fusion.2
  303.7 70.0 %all-reduce.3.cloned.1.call-done = bf16[64,128,128]{2,0,1:T(8,128)(2,1)} async-done(((bf16[64,128,128]{2,0,1:T(8,128)(2,1)}), bf16[64,128,128]{2,0,1:T(8,128)(2,1)}) %all-reduce.3.cloned.1.call-update) | async-done | bytes 2097168 | tf_op jit(solution)/shard_map/psum | solution.py:9
  373.6 21.6 %gather_fusion.1 = bf16[512,64,128]{2,1,0:T(8,128)(2,1)} fusion(bf16[64,128,128]{2,0,1:T(8,128)(2,1)} %all-reduce.3.cloned.1.call-done, s32[1024]{0:T(1024)S(1)} %pad_clamp_fusion), kind=kCustom, calls=%fused_computation.1.clone | custom fusion | bytes 16779264 | tf_op jit(solution)/shard_map/jit(_take)/gather | solution.py:18
  395.3 20.5 %fusion.11 = f32[64,512,128]{2,0,1:T(8,128)} fusion(bf16[1,512,128,128]{3,2,1,0:T(8,128)(2,1)} %param.8, bf16[512,64,128]{2,1,0:T(8,128)(2,1)} %gather_fusion.1, pred[512]{0:T(512)(128)(4,1)S(1)} %compare_and_fusion), kind=kOutput, calls=%fused_computation.11 | convolution fusion | flops 1077936128 | bytes 41943552 | tf_op jit(solution)/shard_map/ksc,src->ksr/dot_general | solution.py:19
  415.7 27.8 %fusion.25 = f32[64,256,128]{1,2,0:T(8,128)} fusion(f32[64,512,128]{2,0,1:T(8,128)} %fusion.11, s32[512]{0:T(512)S(1)} %bitcast.54, pred[512]{0:T(512)(128)(4,1)S(1)} %iota_compare_fusion.1), kind=kOutput, calls=%fused_computation.24 | convolution fusion | flops 12885164032 | bytes 25168384 | tf_op jit(solution)/shard_map/is,ksr->kir/dot_general | solution.py:24
  443.5 9.2 %copy.13 = f32[64,256,128]{2,1,0:T(8,128)} copy(f32[64,256,128]{1,2,0:T(8,128)} %fusion.25) | data formatting | bytes 16777216 | tf_op jit(solution)/shard_map/is,ksr->kir/transpose | solution.py:24
  452.7 11.3 %copy.30 = f32[8,8,256,128]{3,1,2,0:T(8,128)} copy(f32[8,8,256,128]{3,2,1,0:T(8,128)} %bitcast.52) | data formatting | bytes 16777216
  464.0 89.7 %reduce-scatter.2.cloned.1.call-done = f32[64,4096]{1,0:T(8,128)} async-done(((f32[64,32768]{1,0:T(8,128)}), f32[64,4096]{1,0:T(8,128)}) %reduce-scatter.2.cloned.1.call-update) | async-done | bytes 1048592 | tf_op jit(solution)/shard_map/reduce_scatter | solution.py:50
  (12 shorter events, 0.3 us)
Async XLA Ops:
  6.5 367.1 %all-reduce.3.cloned.1.call-start = ((), (), s32[]{:S(2)}) async-start(), calls=%async_computation.1 | async-start | bytes 4194304 | tf_op jit(solution)/shard_map/psum | solution.py:9
  6.5 15.4 %collective-permute-start = (bf16[64,4096]{1,0:T(8,128)(2,1)}, bf16[64,4096]{1,0:T(8,128)(2,1)S(1)}, u32[]{:S(2)}, u32[]{:S(2)}) collective-permute-start(bf16[64,4096]{1,0:T(8,128)(2,1)} %param.7), channel_id=1, source_target_pairs={{0,24},{8,0},{16,8},{24,16},{1,25},{9,1},{17,9},{25,17},{2,26},{10... | collective-permute-start | bytes 1572872 | tf_op jit(solution)/shard_map/ppermute | solution.py:42
  23.1 24.1 %collective-permute-start.1 = (bf16[64,8192]{1,0:T(8,128)(2,1)S(1)}, bf16[64,8192]{1,0:T(8,128)(2,1)S(1)}, u32[]{:S(2)}, u32[]{:S(2)}) collective-permute-start(bf16[64,8192]{1,0:T(8,128)(2,1)S(1)} %pad_maximum_fusion), channel_id=1, source_target_pairs={{0,16},{8,24},{16,0},{24,8},{1,17},{9,25},{17,1},{25,9},{2,18},{10... | collective-permute-start | bytes 3145736 | tf_op jit(solution)/shard_map/ppermute | solution.py:42
  62.5 20.4 %copy-start = (s32[1,512]{1,0:T(1,128)S(1)}, s32[1,512]{1,0:T(1,128)}, u32[]{:S(2)}) copy-start(s32[1,512]{1,0:T(1,128)} %param.9) | copy-start | bytes 6148
  303.6 250.1 %reduce-scatter.2.cloned.1.call-start = ((), (), s32[]{:S(2)}) async-start(), calls=%async_computation.2 | async-start | bytes 9437184 | tf_op jit(solution)/shard_map/reduce_scatter | solution.py:50
Sparse Core Ops, SparseCore 0:
  303.7 69.8 all-reduce.2
  464.2 89.5 reduce-scatter.1
